TPU v7x, 512 devices: a whole 4x8x8 slice. The times are simulated.
512 devices in a mesh: angle: 8 (over x, core), gx: 16 (over y, z_lo), gy: 4 (over z_hi).
Axes of the slice: x: 4, y: 8, z: 8 (z_hi: 4, z_lo: 2; z = z_hi * 2 + z_lo), core: 2. Of those that a mesh axis runs over, the one named last changes fastest.
Arguments:
- forward_fields: float32 [8, 12, 128, 64, 128], P('angle', None, 'gx', 'gy'), may hold values from -6 to 6
- adjoint_fields: float32 [8, 12, 128, 64, 128], P('angle', None, 'gx', 'gy'), may hold values from -6 to 6
- forward_spectrum: float32 [8, 6, 128, 64, 128], P('angle', None, 'gx', 'gy'), may hold values from -6 to 6
- adjoint_spectrum: float32 [8, 6, 128, 64, 128], P('angle', None, 'gx', 'gy'), may hold values from -6 to 6
- permittivity: float32 [128, 64, 128], P('gx', 'gy'), may hold values from 1 to 12
- phase_table: float32 [8, 2], replicated, may hold values from -3.140625 to 3.140625
- angle_index: int32 [8], P('angle'), may hold values from 0 to 7, each once
- design_tiles: int32 [16], replicated, may hold values from 0 to 63, as said below
Outputs:
- forward_transform: float32 [8, 6, 128, 64, 128], P('angle', None, 'gx', 'gy')
- adjoint_transform: float32 [8, 6, 128, 64, 128], P('angle', None, 'gx', 'gy')
- gradient: float32 [128, 64, 128], P('gx', 'gy', 'angle')
Inputs may be any that keep to these rules, and one draw needn't show every extreme that they name: `angle_index`: every row of phase_table is used by exactly one angle. `design_tiles`: 16 distinct tile numbers; tiles 0 and 63 are always among them.
All inputs are finite; a program needn't handle non-finite values.
Results may differ from a plain program's by a relative error of at most 0.0001.
Values sent between devices are 32-bit elements; how exact they have to be, the bound alone decides.
A program may use at most 64 MiB of HBM per device.

v0:
```python
import math
import jax
import jax.numpy as jnp
from jax import lax
from jax.sharding import PartitionSpec as P

STEPS = 3
courant = 0.5
omega_step = 0.7


def from_behind(value, axis, steps):
    count = lax.axis_size(axis)
    pairs = [(source, (source + steps) % count) for source in range(count)]
    return lax.ppermute(value, axis, pairs)


def rotate_runs(pair, cosine, sine):
    sine_full = sine.reshape((2,) + (1,) * (pair.ndim - 2))
    real_part = pair[:, 0]
    imag_part = pair[:, 1]
    return jnp.stack(
        [real_part * cosine - imag_part * sine_full, real_part * sine_full + imag_part * cosine],
        axis=1,
    )


def next_depth(field):
    return jnp.concatenate([field[..., 1:], jnp.zeros_like(field[..., :1])], axis=-1)


def prev_depth(field):
    return jnp.concatenate([jnp.zeros_like(field[..., :1]), field[..., :-1]], axis=-1)


def curl_forward(efield, phases):
    cos_x, sine_x, cos_y, sine_y = phases
    place_x = lax.axis_index("gx")
    place_y = lax.axis_index("gy")
    last_x = lax.axis_size("gx") - 1
    last_y = lax.axis_size("gy") - 1
    send_x = efield[:, :, 1:3, 0]
    got_x = from_behind(send_x, "gx", -1)
    got_x = jnp.where(place_x == last_x, rotate_runs(got_x, cos_x, sine_x), got_x)
    send_y = jnp.stack([efield[:, :, 0, :, 0], efield[:, :, 2, :, 0]], axis=2)
    got_y = from_behind(send_y, "gy", -1)
    got_y = jnp.where(place_y == last_y, rotate_runs(got_y, cos_y, sine_y), got_y)
    comp_x = efield[:, :, 0]
    comp_y = efield[:, :, 1]
    comp_z = efield[:, :, 2]
    dz_dy = jnp.concatenate([comp_z[:, :, :, 1:], got_y[:, :, 1][:, :, :, None]], axis=3) - comp_z
    dy_dz = next_depth(comp_y) - comp_y
    dx_dz = next_depth(comp_x) - comp_x
    dz_dx = jnp.concatenate([comp_z[:, :, 1:], got_x[:, :, 1][:, :, None]], axis=2) - comp_z
    dy_dx = jnp.concatenate([comp_y[:, :, 1:], got_x[:, :, 0][:, :, None]], axis=2) - comp_y
    dx_dy = jnp.concatenate([comp_x[:, :, :, 1:], got_y[:, :, 0][:, :, :, None]], axis=3) - comp_x
    return jnp.stack([dz_dy - dy_dz, dx_dz - dz_dx, dy_dx - dx_dy], axis=2)


def curl_backward(hfield, phases):
    cos_x, sine_x, cos_y, sine_y = phases
    place_x = lax.axis_index("gx")
    place_y = lax.axis_index("gy")
    send_x = hfield[:, :, 1:3, -1]
    got_x = from_behind(send_x, "gx", 1)
    got_x = jnp.where(place_x == 0, rotate_runs(got_x, cos_x, -sine_x), got_x)
    send_y = jnp.stack([hfield[:, :, 0, :, -1], hfield[:, :, 2, :, -1]], axis=2)
    got_y = from_behind(send_y, "gy", 1)
    got_y = jnp.where(place_y == 0, rotate_runs(got_y, cos_y, -sine_y), got_y)
    comp_x = hfield[:, :, 0]
    comp_y = hfield[:, :, 1]
    comp_z = hfield[:, :, 2]
    hz_below_y = jnp.concatenate([got_y[:, :, 1][:, :, :, None], comp_z[:, :, :, :-1]], axis=3)
    hx_below_y = jnp.concatenate([got_y[:, :, 0][:, :, :, None], comp_x[:, :, :, :-1]], axis=3)
    hz_below_x = jnp.concatenate([got_x[:, :, 1][:, :, None], comp_z[:, :, :-1]], axis=2)
    hy_below_x = jnp.concatenate([got_x[:, :, 0][:, :, None], comp_y[:, :, :-1]], axis=2)
    first = comp_z - hz_below_y - (comp_y - prev_depth(comp_y))
    second = comp_x - prev_depth(comp_x) - (comp_z - hz_below_x)
    third = comp_y - hy_below_x - (comp_x - hx_below_y)
    return jnp.stack([first, second, third], axis=2)


def shards(
    forward_fields,
    adjoint_fields,
    forward_spectrum,
    adjoint_spectrum,
    permittivity,
    phase_table,
    angle_index,
    design_tiles,
):
    cells = forward_fields.shape[2:]
    fields = jnp.concatenate([forward_fields, adjoint_fields], axis=0)
    spectrum = jnp.concatenate([forward_spectrum, adjoint_spectrum], axis=0).reshape(
        (2, 2, 3) + cells
    )
    table_rows = phase_table.shape[0]
    picked = (jnp.arange(table_rows) == angle_index[0]).astype(jnp.float32)
    angle_x = jnp.sum(picked * phase_table[:, 0])
    angle_y = jnp.sum(picked * phase_table[:, 1])
    run_sign = jnp.array([1.0, -1.0], jnp.float32)
    efield = fields[:, 0:6].reshape((2, 2, 3) + cells)
    hfield = fields[:, 6:12].reshape((2, 2, 3) + cells)
    phases = (
        jnp.cos(angle_x),
        run_sign * jnp.sin(angle_x),
        jnp.cos(angle_y),
        run_sign * jnp.sin(angle_y),
    )
    coef = courant / permittivity
    for step in range(STEPS):
        hfield = hfield - courant * curl_forward(efield, phases)
        efield = efield + coef * curl_backward(hfield, phases)
        theta = omega_step * (step + 1)
        spectrum = spectrum + rotate_runs(
            efield, math.cos(theta), jnp.full((2,), math.sin(theta), jnp.float32)
        )
    local_term = jnp.sum(spectrum[0, 0] * spectrum[1, 0] - spectrum[0, 1] * spectrum[1, 1], axis=0)
    own_tile = lax.axis_index("gx") * lax.axis_size("gy") + lax.axis_index("gy")
    chosen = jnp.any(design_tiles == own_tile)
    local_term = jnp.where(chosen, local_term, jnp.zeros_like(local_term))
    groups = lax.axis_size("angle")
    whole = lax.psum(local_term, "angle")
    share = whole.shape[2] // groups
    summed = lax.dynamic_slice_in_dim(whole, lax.axis_index("angle") * share, share, 2)
    gradient = summed * (1.0 / groups)
    forward_out = spectrum[0].reshape((1, 6) + cells)
    adjoint_out = spectrum[1].reshape((1, 6) + cells)
    return (forward_out, adjoint_out, gradient)


def solution(mesh):
    in_specs = (
        P("angle", None, "gx", "gy", None),
        P("angle", None, "gx", "gy", None),
        P("angle", None, "gx", "gy", None),
        P("angle", None, "gx", "gy", None),
        P("gx", "gy", None),
        P(),
        P("angle"),
        P(),
    )
    out_specs = (
        P("angle", None, "gx", "gy", None),
        P("angle", None, "gx", "gy", None),
        P("gx", "gy", "angle"),
    )
    return jax.shard_map(shards, mesh=mesh, in_specs=in_specs, out_specs=out_specs, check_vma=False)
```

profile of v0, /device:TPU:8, one launch (start us, length us, event | category | flops | bytes accessed | tf_op | source)
XLA Modules:
  0.0 201.6 jit_solution(371373391882974185)
XLA Ops:
  9.4 11.1 %collective-permute-start = (f32[2,2,2,8,128]{4,1,0,3,2:T(2,128)}, f32[2,2,2,8,128]{4,1,0,3,2:T(2,128)}, u32[]{:S(2)}, u32[]{:S(2)}) collective-permute-start(f32[2,2,2,8,128]{4,1,0,3,2:T(2,128)} %pad_maximum_fusion.1), channel_id=1, source_target_pairs={{0,3},{1,0},{2,1},{3,2},{4,7},{5,4},{6,5},{7,6},{8,11},{9,8},{10,9... | collective-permute-start | bytes 98312 | tf_op jit(solution)/shard_map/ppermute | solution.py:15
  21.8 3.3 %collective-permute-start.1 = (f32[2,2,2,16,128]{4,1,0,3,2:T(2,128)}, f32[2,2,2,16,128]{4,1,0,3,2:T(2,128)S(1)}, u32[]{:S(2)}, u32[]{:S(2)}) collective-permute-start(f32[2,2,2,16,128]{4,1,0,3,2:T(2,128)} %slice_bitcast_fusion.25), channel_id=1, source_target_pairs={{0,60},{4,0},{8,4},{12,8},{16,12},{20,16},{24,20},{28,24},{32,28},... | collective-permute-start | bytes 196616 | tf_op jit(solution)/shard_map/ppermute | solution.py:15
  35.7 2.0 %slice.554 = f32[2,2,8,16,127]{4,1,0,3,2:T(2,128)} slice(f32[2,2,8,16,128]{4,1,0,3,2:T(2,128)} %copy-done.4), slice={[0:2], [0:2], [0:8], [0:16], [1:128]} | slice | bytes 520192 | tf_op jit(solution)/shard_map/slice | solution.py:29
  37.8 1.7 slice.547
  39.4 1.6 slice.557
  44.2 1.4 fusion.11
  47.5 2.6 %collective-permute-start.3 = (f32[2,2,2,16,128]{4,1,0,3,2:T(2,128)S(1)}, f32[2,2,2,16,128]{4,1,0,3,2:T(2,128)S(1)}, u32[]{:S(2)}, u32[]{:S(2)}) collective-permute-start(f32[2,2,2,16,128]{4,1,0,3,2:T(2,128)S(1)} %slice_bitcast_fusion.24), channel_id=1, source_target_pairs={{0,4},{4,8},{8,12},{12,16},{16,20},{20,24},{24,28},{28,32},{32,36}... | collective-permute-start | bytes 196616 | tf_op jit(solution)/shard_map/ppermute | solution.py:15
  50.1 1.9 collective-permute-start.2
  52.1 5.9 %collective-permute-done.2 = f32[2,2,2,8,128]{4,1,0,3,2:T(2,128)S(1)} collective-permute-done((f32[2,2,2,8,128]{4,1,0,3,2:T(2,128)S(1)}, f32[2,2,2,8,128]{4,1,0,3,2:T(2,128)S(1)}, u32[]{:S(2)}, u32[]{:S(2)}) %collective-permute-start.2) | collective-permute-done | bytes 32800 | tf_op jit(solution)/shard_map/ppermute | solution.py:15
  61.9 1.9 collective-permute-start.4
  64.6 4.5 %collective-permute-start.5 = (f32[2,2,2,16,128]{4,1,0,3,2:T(2,128)S(1)}, f32[2,2,2,16,128]{4,1,0,3,2:T(2,128)S(1)}, u32[]{:S(2)}, u32[]{:S(2)}) collective-permute-start(f32[2,2,2,16,128]{4,1,0,3,2:T(2,128)S(1)} %slice_bitcast_fusion.23), channel_id=1, source_target_pairs={{0,60},{4,0},{8,4},{12,8},{16,12},{20,16},{24,20},{28,24},{32,28},... | collective-permute-start | bytes 196616 | tf_op jit(solution)/shard_map/ppermute | solution.py:15
  69.2 1.9 collective-permute-done.5
  74.2 4.8 %collective-permute-start.6 = (f32[2,2,2,8,128]{4,3,2,1,0:T(8,128)S(1)}, f32[2,2,2,8,128]{4,3,2,1,0:T(8,128)S(1)}, u32[]{:S(2)}, u32[]{:S(2)}) collective-permute-start(f32[2,2,2,8,128]{4,3,2,1,0:T(8,128)S(1)} %pad_maximum_fusion.4), channel_id=1, source_target_pairs={{0,1},{1,2},{2,3},{3,0},{4,5},{5,6},{6,7},{7,4},{8,9},{9,10},{10,1... | collective-permute-start | bytes 98312 | tf_op jit(solution)/shard_map/ppermute | solution.py:15
  79.0 4.8 %collective-permute-start.7 = (f32[2,2,2,16,128]{4,1,0,3,2:T(2,128)S(1)}, f32[2,2,2,16,128]{4,1,0,3,2:T(2,128)S(1)}, u32[]{:S(2)}, u32[]{:S(2)}) collective-permute-start(f32[2,2,2,16,128]{4,1,0,3,2:T(2,128)S(1)} %bitcast.365), channel_id=1, source_target_pairs={{0,4},{4,8},{8,12},{12,16},{16,20},{20,24},{24,28},{28,32},{32,36}... | collective-permute-start | bytes 196616 | tf_op jit(solution)/shard_map/ppermute | solution.py:15
  84.3 1.7 collective-permute-done.7
  89.9 3.1 %collective-permute-start.8 = (f32[2,2,2,8,128]{4,1,0,3,2:T(2,128)S(1)}, f32[2,2,2,8,128]{4,1,0,3,2:T(2,128)S(1)}, u32[]{:S(2)}, u32[]{:S(2)}) collective-permute-start(f32[2,2,2,8,128]{4,1,0,3,2:T(2,128)S(1)} %pad_maximum_fusion.5), channel_id=1, source_target_pairs={{0,3},{1,0},{2,1},{3,2},{4,7},{5,4},{6,5},{7,6},{8,11},{9,8},{10,9... | collective-permute-start | bytes 98312 | tf_op jit(solution)/shard_map/ppermute | solution.py:15
  93.7 4.7 %collective-permute-start.9 = (f32[2,2,2,16,128]{4,1,0,3,2:T(2,128)S(1)}, f32[2,2,2,16,128]{4,1,0,3,2:T(2,128)S(1)}, u32[]{:S(2)}, u32[]{:S(2)}) collective-permute-start(f32[2,2,2,16,128]{4,1,0,3,2:T(2,128)S(1)} %slice_bitcast_fusion.22), channel_id=1, source_target_pairs={{0,60},{4,0},{8,4},{12,8},{16,12},{20,16},{24,20},{28,24},{32,28},... | collective-permute-start | bytes 196616 | tf_op jit(solution)/shard_map/ppermute | solution.py:15
  98.6 1.7 collective-permute-done.9
  102.9 3.6 %collective-permute-start.10 = (f32[2,2,2,8,128]{4,3,2,1,0:T(8,128)S(1)}, f32[2,2,2,8,128]{4,3,2,1,0:T(8,128)S(1)}, u32[]{:S(2)}, u32[]{:S(2)}) collective-permute-start(f32[2,2,2,8,128]{4,3,2,1,0:T(8,128)S(1)} %copy.222), channel_id=1, source_target_pairs={{0,1},{1,2},{2,3},{3,0},{4,5},{5,6},{6,7},{7,4},{8,9},{9,10},{10,1... | collective-permute-start | bytes 98312 | tf_op jit(solution)/shard_map/ppermute | solution.py:15
  106.5 4.6 %collective-permute-start.11 = (f32[2,2,2,16,128]{4,1,0,3,2:T(2,128)S(1)}, f32[2,2,2,16,128]{4,1,0,3,2:T(2,128)S(1)}, u32[]{:S(2)}, u32[]{:S(2)}) collective-permute-start(f32[2,2,2,16,128]{4,1,0,3,2:T(2,128)S(1)} %bitcast.364), channel_id=1, source_target_pairs={{0,4},{4,8},{8,12},{12,16},{16,20},{20,24},{24,28},{28,32},{32,36}... | collective-permute-start | bytes 196616 | tf_op jit(solution)/shard_map/ppermute | solution.py:15
  111.6 3.5 %collective-permute-done.11 = f32[2,2,2,16,128]{4,1,0,3,2:T(2,128)S(1)} collective-permute-done((f32[2,2,2,16,128]{4,1,0,3,2:T(2,128)S(1)}, f32[2,2,2,16,128]{4,1,0,3,2:T(2,128)S(1)}, u32[]{:S(2)}, u32[]{:S(2)}) %collective-permute-start.11) | collective-permute-done | bytes 65568 | tf_op jit(solution)/shard_map/ppermute | solution.py:15
  118.9 2.4 %fusion.3 = f32[2,2,3,8,16,128]{5,1,0,4,2,3:T(2,128)S(1)} fusion(f32[2,1,3,8,16,128]{5,1,0,4,2,3:T(1,128)S(1)} %get-tuple-element.40, f32[2,1,3,8,16,128]{5,1,0,4,2,3:T(1,128)S(1)} %get-tuple-element.39, f32[2,1,3,8,16,128]{5,1,0,4,2,3:T(1,128)S(1)} %get-tuple-element.25, f32[2,1,3,8,16,128]{5,1,0,4,2,3:T(1,128)S(1)} %get-tuple-element.24, ...), kind=kLoop, calls=%fused_computation.7 | loop fusion | flops 1179648 | bytes 3932160 | tf_op jit(solution)/shard_map/add | solution.py:116
  125.1 68.1 %all-reduce.14.cloned.1.call-done = f32[8,16,128]{2,1,0:T(8,128)} async-done(((f32[8,16,128]{2,1,0:T(8,128)}), f32[8,16,128]{2,1,0:T(8,128)}) %all-reduce.14.cloned.1.call-update) | async-done | bytes 65552 | tf_op jit(solution)/shard_map/psum | solution.py:124
  193.2 1.6 dynamic-slice_multiply_fusion
  (168 shorter events, 38.7 us)
Async XLA Ops:
  7.2 1.4 copy-start.9
  7.2 186.1 %all-reduce.14.cloned.1.call-start = ((), (), s32[]{:S(2)}) async-start(), calls=%async_computation | async-start | bytes 131072 | tf_op jit(solution)/shard_map/psum | solution.py:124
  9.4 16.4 %copy-start.10 = (f32[8,2]{0,1:T(2,128)S(1)}, f32[8,2]{0,1:T(2,128)}, u32[]{:S(2)}) copy-start(f32[8,2]{0,1:T(2,128)} %param.14) | copy-start | bytes 196
  9.4 32.7 %collective-permute-start = (f32[2,2,2,8,128]{4,1,0,3,2:T(2,128)}, f32[2,2,2,8,128]{4,1,0,3,2:T(2,128)}, u32[]{:S(2)}, u32[]{:S(2)}) collective-permute-start(f32[2,2,2,8,128]{4,1,0,3,2:T(2,128)} %pad_maximum_fusion.1), channel_id=1, source_target_pairs={{0,3},{1,0},{2,1},{3,2},{4,7},{5,4},{6,5},{7,6},{8,11},{9,8},{10,9... | collective-permute-start | bytes 98312 | tf_op jit(solution)/shard_map/ppermute | solution.py:15
  21.8 22.2 %collective-permute-start.1 = (f32[2,2,2,16,128]{4,1,0,3,2:T(2,128)}, f32[2,2,2,16,128]{4,1,0,3,2:T(2,128)S(1)}, u32[]{:S(2)}, u32[]{:S(2)}) collective-permute-start(f32[2,2,2,16,128]{4,1,0,3,2:T(2,128)} %slice_bitcast_fusion.25), channel_id=1, source_target_pairs={{0,60},{4,0},{8,4},{12,8},{16,12},{20,16},{24,20},{28,24},{32,28},... | collective-permute-start | bytes 196616 | tf_op jit(solution)/shard_map/ppermute | solution.py:15
  25.1 5.3 %copy-start = (f32[2,2,1,8,16,128]{5,4,3,2,1,0:T(8,128)}, f32[2,2,1,8,16,128]{5,4,3,2,1,0:T(8,128)S(1)}, u32[]{:S(2)}) copy-start(f32[2,2,1,8,16,128]{5,4,3,2,1,0:T(8,128)S(1)} %get-tuple-element.49) | copy-start | bytes 786436
  25.1 5.2 %copy-start.2 = (f32[2,2,8,16,128]{4,1,0,3,2:T(2,128)}, f32[2,2,8,16,128]{4,1,0,3,2:T(2,128)S(1)}, u32[]{:S(2)}) copy-start(f32[2,2,8,16,128]{4,1,0,3,2:T(2,128)S(1)} %slice_bitcast_fusion.21) | copy-start | bytes 786436
  28.9 1.5 copy-start.4
  35.7 5.3 %copy-start.3 = (f32[2,2,8,16,128]{4,1,0,3,2:T(2,128)S(1)}, f32[2,2,8,16,128]{4,1,0,3,2:T(2,128)}, u32[]{:S(2)}) copy-start(f32[2,2,8,16,128]{4,1,0,3,2:T(2,128)} %copy-done.2) | copy-start | bytes 786436
  42.1 3.5 %copy-start.1 = (f32[2,2,1,8,16,128]{5,4,3,2,1,0:T(8,128)S(1)}, f32[2,2,1,8,16,128]{5,4,3,2,1,0:T(8,128)}, u32[]{:S(2)}) copy-start(f32[2,2,1,8,16,128]{5,4,3,2,1,0:T(8,128)} %copy-done) | copy-start | bytes 786436
  42.1 3.5 %copy-start.5 = (f32[2,2,8,16,127]{4,1,0,3,2:T(2,128)S(1)}, f32[2,2,8,16,127]{4,1,0,3,2:T(2,128)}, u32[]{:S(2)}) copy-start(f32[2,2,8,16,127]{4,1,0,3,2:T(2,128)} %slice.554) | copy-start | bytes 780292
  42.1 3.5 %copy-start.6 = (f32[2,2,8,16,127]{4,1,0,3,2:T(2,128)S(1)}, f32[2,2,8,16,127]{4,1,0,3,2:T(2,128)}, u32[]{:S(2)}) copy-start(f32[2,2,8,16,127]{4,1,0,3,2:T(2,128)} %slice.556) | copy-start | bytes 780292
  42.1 3.5 %copy-start.7 = (f32[2,2,8,15,128]{4,1,0,3,2:T(2,128)S(1)}, f32[2,2,8,15,128]{4,1,0,3,2:T(2,128)}, u32[]{:S(2)}) copy-start(f32[2,2,8,15,128]{4,1,0,3,2:T(2,128)} %slice.547) | copy-start | bytes 737284
  42.1 3.5 %copy-start.8 = (f32[2,2,7,16,128]{4,1,0,3,2:T(2,128)S(1)}, f32[2,2,7,16,128]{4,1,0,3,2:T(2,128)}, u32[]{:S(2)}) copy-start(f32[2,2,7,16,128]{4,1,0,3,2:T(2,128)} %slice.557) | copy-start | bytes 688132
  47.5 10.7 %collective-permute-start.3 = (f32[2,2,2,16,128]{4,1,0,3,2:T(2,128)S(1)}, f32[2,2,2,16,128]{4,1,0,3,2:T(2,128)S(1)}, u32[]{:S(2)}, u32[]{:S(2)}) collective-permute-start(f32[2,2,2,16,128]{4,1,0,3,2:T(2,128)S(1)} %slice_bitcast_fusion.24), channel_id=1, source_target_pairs={{0,4},{4,8},{8,12},{12,16},{16,20},{20,24},{24,28},{28,32},{32,36}... | collective-permute-start | bytes 196616 | tf_op jit(solution)/shard_map/ppermute | solution.py:15
  50.1 7.9 %collective-permute-start.2 = (f32[2,2,2,8,128]{4,1,0,3,2:T(2,128)S(1)}, f32[2,2,2,8,128]{4,1,0,3,2:T(2,128)S(1)}, u32[]{:S(2)}, u32[]{:S(2)}) collective-permute-start(f32[2,2,2,8,128]{4,1,0,3,2:T(2,128)S(1)} %pad_maximum_fusion.2), channel_id=1, source_target_pairs={{0,1},{1,2},{2,3},{3,0},{4,5},{5,6},{6,7},{7,4},{8,9},{9,10},{10,1... | collective-permute-start | bytes 98312 | tf_op jit(solution)/shard_map/ppermute | solution.py:15
  61.9 7.1 %collective-permute-start.4 = (f32[2,2,2,8,128]{4,1,0,3,2:T(2,128)S(1)}, f32[2,2,2,8,128]{4,1,0,3,2:T(2,128)S(1)}, u32[]{:S(2)}, u32[]{:S(2)}) collective-permute-start(f32[2,2,2,8,128]{4,1,0,3,2:T(2,128)S(1)} %pad_maximum_fusion.3), channel_id=1, source_target_pairs={{0,3},{1,0},{2,1},{3,2},{4,7},{5,4},{6,5},{7,6},{8,11},{9,8},{10,9... | collective-permute-start | bytes 98312 | tf_op jit(solution)/shard_map/ppermute | solution.py:15
  64.6 6.5 %collective-permute-start.5 = (f32[2,2,2,16,128]{4,1,0,3,2:T(2,128)S(1)}, f32[2,2,2,16,128]{4,1,0,3,2:T(2,128)S(1)}, u32[]{:S(2)}, u32[]{:S(2)}) collective-permute-start(f32[2,2,2,16,128]{4,1,0,3,2:T(2,128)S(1)} %slice_bitcast_fusion.23), channel_id=1, source_target_pairs={{0,60},{4,0},{8,4},{12,8},{16,12},{20,16},{24,20},{28,24},{32,28},... | collective-permute-start | bytes 196616 | tf_op jit(solution)/shard_map/ppermute | solution.py:15
  74.2 10.0 %collective-permute-start.6 = (f32[2,2,2,8,128]{4,3,2,1,0:T(8,128)S(1)}, f32[2,2,2,8,128]{4,3,2,1,0:T(8,128)S(1)}, u32[]{:S(2)}, u32[]{:S(2)}) collective-permute-start(f32[2,2,2,8,128]{4,3,2,1,0:T(8,128)S(1)} %pad_maximum_fusion.4), channel_id=1, source_target_pairs={{0,1},{1,2},{2,3},{3,0},{4,5},{5,6},{6,7},{7,4},{8,9},{9,10},{10,1... | collective-permute-start | bytes 98312 | tf_op jit(solution)/shard_map/ppermute | solution.py:15
  79.0 7.1 %collective-permute-start.7 = (f32[2,2,2,16,128]{4,1,0,3,2:T(2,128)S(1)}, f32[2,2,2,16,128]{4,1,0,3,2:T(2,128)S(1)}, u32[]{:S(2)}, u32[]{:S(2)}) collective-permute-start(f32[2,2,2,16,128]{4,1,0,3,2:T(2,128)S(1)} %bitcast.365), channel_id=1, source_target_pairs={{0,4},{4,8},{8,12},{12,16},{16,20},{20,24},{24,28},{28,32},{32,36}... | collective-permute-start | bytes 196616 | tf_op jit(solution)/shard_map/ppermute | solution.py:15
  89.9 8.6 %collective-permute-start.8 = (f32[2,2,2,8,128]{4,1,0,3,2:T(2,128)S(1)}, f32[2,2,2,8,128]{4,1,0,3,2:T(2,128)S(1)}, u32[]{:S(2)}, u32[]{:S(2)}) collective-permute-start(f32[2,2,2,8,128]{4,1,0,3,2:T(2,128)S(1)} %pad_maximum_fusion.5), channel_id=1, source_target_pairs={{0,3},{1,0},{2,1},{3,2},{4,7},{5,4},{6,5},{7,6},{8,11},{9,8},{10,9... | collective-permute-start | bytes 98312 | tf_op jit(solution)/shard_map/ppermute | solution.py:15
  93.7 6.6 %collective-permute-start.9 = (f32[2,2,2,16,128]{4,1,0,3,2:T(2,128)S(1)}, f32[2,2,2,16,128]{4,1,0,3,2:T(2,128)S(1)}, u32[]{:S(2)}, u32[]{:S(2)}) collective-permute-start(f32[2,2,2,16,128]{4,1,0,3,2:T(2,128)S(1)} %slice_bitcast_fusion.22), channel_id=1, source_target_pairs={{0,60},{4,0},{8,4},{12,8},{16,12},{20,16},{24,20},{28,24},{32,28},... | collective-permute-start | bytes 196616 | tf_op jit(solution)/shard_map/ppermute | solution.py:15
  102.9 8.6 %collective-permute-start.10 = (f32[2,2,2,8,128]{4,3,2,1,0:T(8,128)S(1)}, f32[2,2,2,8,128]{4,3,2,1,0:T(8,128)S(1)}, u32[]{:S(2)}, u32[]{:S(2)}) collective-permute-start(f32[2,2,2,8,128]{4,3,2,1,0:T(8,128)S(1)} %copy.222), channel_id=1, source_target_pairs={{0,1},{1,2},{2,3},{3,0},{4,5},{5,6},{6,7},{7,4},{8,9},{9,10},{10,1... | collective-permute-start | bytes 98312 | tf_op jit(solution)/shard_map/ppermute | solution.py:15
  106.5 8.6 %collective-permute-start.11 = (f32[2,2,2,16,128]{4,1,0,3,2:T(2,128)S(1)}, f32[2,2,2,16,128]{4,1,0,3,2:T(2,128)S(1)}, u32[]{:S(2)}, u32[]{:S(2)}) collective-permute-start(f32[2,2,2,16,128]{4,1,0,3,2:T(2,128)S(1)} %bitcast.364), channel_id=1, source_target_pairs={{0,4},{4,8},{8,12},{12,16},{16,20},{20,24},{24,28},{28,32},{32,36}... | collective-permute-start | bytes 196616 | tf_op jit(solution)/shard_map/ppermute | solution.py:15
Sparse Core Ops, SparseCore 0:
  123.2 69.9 all-reduce.13
where the time goes:
time: 202 us
  waiting for transfers between devices  82.9 us (41%)
  starting transfers between devices  50.9 us (25%)
  other arithmetic  31.9 us (16%)
  between operations  18.5 us (9%)
  local copies, waits for them, and re-layouts  17.4 us (9%)
    psum x1, waiting for transfers between devices, shards(): whole = lax.psum(local_term, 'angle')  68.1 us
    ppermute x12, starting transfers between devices, from_behind(): return lax.ppermute(value, axis, pairs)  50.9 us
    ppermute x12, waiting for transfers between devices, from_behind(): return lax.ppermute(value, axis, pairs)  14.8 us
    sub x15, other arithmetic, rotate_runs(): real_part * cosine - imag_part * sine_full  5.45 us
    slice x6, local copies, waits for them, and re-layouts, next_depth(): field[..., 1:]  4.42 us
  transfers between devices with their start and end apart: 13, of which 6 were waited for; matrix products, arithmetic and copies ran while one was open for 11% of the time, Pallas kernels for 0%

commit v1 on v0

--- a/solution.py
+++ b/solution.py
@@ -121,7 +121,7 @@
     chosen = jnp.any(design_tiles == own_tile)
     local_term = jnp.where(chosen, local_term, jnp.zeros_like(local_term))
     groups = lax.axis_size("angle")
-    whole = lax.psum(local_term, "angle")
+    whole = jnp.sum(lax.all_gather(local_term, "angle"), axis=0)
     share = whole.shape[2] // groups
     summed = lax.dynamic_slice_in_dim(whole, lax.axis_index("angle") * share, share, 2)
     gradient = summed * (1.0 / groups)

time: 202 us -> 139 us (0.69)
  the two profiles are of different devices: /device:TPU:8 before, /device:TPU:1 now
where the time goes in v1:
time: 139 us; the launch traced here: 138 us
  starting transfers between devices  46.9 us (34%)
  other arithmetic  30.4 us (22%)
  blocking collectives  21.1 us (15%)
  local copies, waits for them, and re-layouts  17.4 us (13%)
  waiting for transfers between devices  17.1 us (12%)
  between operations  5.17 us (4%)
    ppermute x12, starting transfers between devices, from_behind(): return lax.ppermute(value, axis, pairs)  46.9 us
    all_gather x1, blocking collectives, shards(): whole = jnp.sum(lax.all_gather(local_term, 'angle'), axis=0)  21.1 us
    ppermute x12, waiting for transfers between devices, from_behind(): return lax.ppermute(value, axis, pairs)  17.1 us
    sub x15, other arithmetic, rotate_runs(): real_part * cosine - imag_part * sine_full  5.45 us
    slice x6, local copies, waits for them, and re-layouts, next_depth(): field[..., 1:]  4.43 us
    add x3, other arithmetic, shards(): efield = efield + coef * curl_backward(hfield, phases)  3.17 us
  transfers between devices with their start and end apart: 12, of which 7 were waited for; matrix products, arithmetic and copies ran while one was open for 14% of the time, Pallas kernels for 0%

profile of v1, /device:TPU:1, one launch (start us, length us, event | category | flops | bytes accessed | tf_op | source)
XLA Modules:
  0.0 138.1 jit_solution(17330058090364904674)
XLA Ops:
  0.6 1.3 constant_dynamic-update-slice_fusion.1
  2.9 11.6 %collective-permute-start = (f32[2,2,2,8,128]{4,1,0,3,2:T(2,128)}, f32[2,2,2,8,128]{4,1,0,3,2:T(2,128)}, u32[]{:S(2)}, u32[]{:S(2)}) collective-permute-start(f32[2,2,2,8,128]{4,1,0,3,2:T(2,128)} %pad_maximum_fusion.1), channel_id=1, source_target_pairs={{0,3},{1,0},{2,1},{3,2},{4,7},{5,4},{6,5},{7,6},{8,11},{9,8},{10,9... | collective-permute-start | bytes 98312 | tf_op jit(solution)/shard_map/ppermute | solution.py:15
  15.7 6.0 %collective-permute-start.1 = (f32[2,2,2,16,128]{4,1,0,3,2:T(2,128)}, f32[2,2,2,16,128]{4,1,0,3,2:T(2,128)S(1)}, u32[]{:S(2)}, u32[]{:S(2)}) collective-permute-start(f32[2,2,2,16,128]{4,1,0,3,2:T(2,128)} %slice_bitcast_fusion.25), channel_id=1, source_target_pairs={{0,60},{4,0},{8,4},{12,8},{16,12},{20,16},{24,20},{28,24},{32,28},... | collective-permute-start | bytes 196616 | tf_op jit(solution)/shard_map/ppermute | solution.py:15
  29.9 1.3 compare_reduce_fusion
  32.5 2.0 %slice.554 = f32[2,2,8,16,127]{4,1,0,3,2:T(2,128)} slice(f32[2,2,8,16,128]{4,1,0,3,2:T(2,128)} %copy-done.4), slice={[0:2], [0:2], [0:8], [0:16], [1:128]} | slice | bytes 520192 | tf_op jit(solution)/shard_map/slice | solution.py:29
  34.6 1.7 %slice.547 = f32[2,2,8,15,128]{4,1,0,3,2:T(2,128)} slice(f32[2,2,8,16,128]{4,1,0,3,2:T(2,128)} %get-tuple-element.111), slice={[0:2], [0:2], [0:8], [1:16], [0:128]} | slice | bytes 491520 | tf_op jit(solution)/shard_map/slice | solution.py:51
  36.2 1.6 %slice.557 = f32[2,2,7,16,128]{4,1,0,3,2:T(2,128)} slice(f32[2,2,8,16,128]{4,1,0,3,2:T(2,128)} %get-tuple-element.111), slice={[0:2], [0:2], [1:8], [0:16], [0:128]} | slice | bytes 458752 | tf_op jit(solution)/shard_map/slice | solution.py:54
  41.0 1.4 %fusion.11 = f32[2,2,1,8,16,128]{5,1,0,4,2,3:T(2,128)S(1)} fusion(f32[2,2,1,1,16,128]{5,1,0,4,3,2:T(2,128)S(1)} %get-tuple-element.82, f32[2,2,1,7,16,128]{5,1,0,4,3,2:T(2,128)} %slice_bitcast_fusion.14, f32[2,2,1,8,1,128]{5,1,0,4,3,2:T(2,128)S(1)} %get-tuple-element.106, f32[2,2,1,8,15,128]{5,1,0,4,3,2:T(2,128)} %slice_bitcast_fusion.8, ...), kind=kLoop, calls=%fused_computation.33 | loop fusion | flops 327680 | bytes 1310720 | tf_op jit(solution)/shard_map/sub | solution.py:57
  44.3 1.9 %collective-permute-start.3 = (f32[2,2,2,16,128]{4,1,0,3,2:T(2,128)S(1)}, f32[2,2,2,16,128]{4,1,0,3,2:T(2,128)S(1)}, u32[]{:S(2)}, u32[]{:S(2)}) collective-permute-start(f32[2,2,2,16,128]{4,1,0,3,2:T(2,128)S(1)} %slice_bitcast_fusion.24), channel_id=1, source_target_pairs={{0,4},{4,8},{8,12},{12,16},{16,20},{20,24},{24,28},{28,32},{32,36}... | collective-permute-start | bytes 196616 | tf_op jit(solution)/shard_map/ppermute | solution.py:15
  46.3 1.9 %collective-permute-start.2 = (f32[2,2,2,8,128]{4,1,0,3,2:T(2,128)S(1)}, f32[2,2,2,8,128]{4,1,0,3,2:T(2,128)S(1)}, u32[]{:S(2)}, u32[]{:S(2)}) collective-permute-start(f32[2,2,2,8,128]{4,1,0,3,2:T(2,128)S(1)} %pad_maximum_fusion.2), channel_id=1, source_target_pairs={{0,1},{1,2},{2,3},{3,0},{4,5},{5,6},{6,7},{7,4},{8,9},{9,10},{10,1... | collective-permute-start | bytes 98312 | tf_op jit(solution)/shard_map/ppermute | solution.py:15
  48.2 5.1 %collective-permute-done.2 = f32[2,2,2,8,128]{4,1,0,3,2:T(2,128)S(1)} collective-permute-done((f32[2,2,2,8,128]{4,1,0,3,2:T(2,128)S(1)}, f32[2,2,2,8,128]{4,1,0,3,2:T(2,128)S(1)}, u32[]{:S(2)}, u32[]{:S(2)}) %collective-permute-start.2) | collective-permute-done | bytes 32800 | tf_op jit(solution)/shard_map/ppermute | solution.py:15
  57.2 1.9 %collective-permute-start.4 = (f32[2,2,2,8,128]{4,1,0,3,2:T(2,128)S(1)}, f32[2,2,2,8,128]{4,1,0,3,2:T(2,128)S(1)}, u32[]{:S(2)}, u32[]{:S(2)}) collective-permute-start(f32[2,2,2,8,128]{4,1,0,3,2:T(2,128)S(1)} %pad_maximum_fusion.3), channel_id=1, source_target_pairs={{0,3},{1,0},{2,1},{3,2},{4,7},{5,4},{6,5},{7,6},{8,11},{9,8},{10,9... | collective-permute-start | bytes 98312 | tf_op jit(solution)/shard_map/ppermute | solution.py:15
  59.9 5.4 %collective-permute-start.5 = (f32[2,2,2,16,128]{4,1,0,3,2:T(2,128)S(1)}, f32[2,2,2,16,128]{4,1,0,3,2:T(2,128)S(1)}, u32[]{:S(2)}, u32[]{:S(2)}) collective-permute-start(f32[2,2,2,16,128]{4,1,0,3,2:T(2,128)S(1)} %slice_bitcast_fusion.23), channel_id=1, source_target_pairs={{0,60},{4,0},{8,4},{12,8},{16,12},{20,16},{24,20},{28,24},{32,28},... | collective-permute-start | bytes 196616 | tf_op jit(solution)/shard_map/ppermute | solution.py:15
  69.5 4.3 %collective-permute-start.6 = (f32[2,2,2,8,128]{4,3,2,1,0:T(8,128)S(1)}, f32[2,2,2,8,128]{4,3,2,1,0:T(8,128)S(1)}, u32[]{:S(2)}, u32[]{:S(2)}) collective-permute-start(f32[2,2,2,8,128]{4,3,2,1,0:T(8,128)S(1)} %pad_maximum_fusion.4), channel_id=1, source_target_pairs={{0,1},{1,2},{2,3},{3,0},{4,5},{5,6},{6,7},{7,4},{8,9},{9,10},{10,1... | collective-permute-start | bytes 98312 | tf_op jit(solution)/shard_map/ppermute | solution.py:15
  73.7 1.9 %collective-permute-start.7 = (f32[2,2,2,16,128]{4,1,0,3,2:T(2,128)S(1)}, f32[2,2,2,16,128]{4,1,0,3,2:T(2,128)S(1)}, u32[]{:S(2)}, u32[]{:S(2)}) collective-permute-start(f32[2,2,2,16,128]{4,1,0,3,2:T(2,128)S(1)} %bitcast.367), channel_id=1, source_target_pairs={{0,4},{4,8},{8,12},{12,16},{16,20},{20,24},{24,28},{28,32},{32,36}... | collective-permute-start | bytes 196616 | tf_op jit(solution)/shard_map/ppermute | solution.py:15
  76.4 4.8 %collective-permute-done.7 = f32[2,2,2,16,128]{4,1,0,3,2:T(2,128)S(1)} collective-permute-done((f32[2,2,2,16,128]{4,1,0,3,2:T(2,128)S(1)}, f32[2,2,2,16,128]{4,1,0,3,2:T(2,128)S(1)}, u32[]{:S(2)}, u32[]{:S(2)}) %collective-permute-start.7) | collective-permute-done | bytes 65568 | tf_op jit(solution)/shard_map/ppermute | solution.py:15
  85.0 3.1 %collective-permute-start.8 = (f32[2,2,2,8,128]{4,1,0,3,2:T(2,128)S(1)}, f32[2,2,2,8,128]{4,1,0,3,2:T(2,128)S(1)}, u32[]{:S(2)}, u32[]{:S(2)}) collective-permute-start(f32[2,2,2,8,128]{4,1,0,3,2:T(2,128)S(1)} %pad_maximum_fusion.5), channel_id=1, source_target_pairs={{0,3},{1,0},{2,1},{3,2},{4,7},{5,4},{6,5},{7,6},{8,11},{9,8},{10,9... | collective-permute-start | bytes 98312 | tf_op jit(solution)/shard_map/ppermute | solution.py:15
  88.9 3.6 %collective-permute-start.9 = (f32[2,2,2,16,128]{4,1,0,3,2:T(2,128)S(1)}, f32[2,2,2,16,128]{4,1,0,3,2:T(2,128)S(1)}, u32[]{:S(2)}, u32[]{:S(2)}) collective-permute-start(f32[2,2,2,16,128]{4,1,0,3,2:T(2,128)S(1)} %slice_bitcast_fusion.22), channel_id=1, source_target_pairs={{0,60},{4,0},{8,4},{12,8},{16,12},{20,16},{24,20},{28,24},{32,28},... | collective-permute-start | bytes 196616 | tf_op jit(solution)/shard_map/ppermute | solution.py:15
  96.5 3.1 %collective-permute-start.10 = (f32[2,2,2,8,128]{4,3,2,1,0:T(8,128)S(1)}, f32[2,2,2,8,128]{4,3,2,1,0:T(8,128)S(1)}, u32[]{:S(2)}, u32[]{:S(2)}) collective-permute-start(f32[2,2,2,8,128]{4,3,2,1,0:T(8,128)S(1)} %copy.293), channel_id=1, source_target_pairs={{0,1},{1,2},{2,3},{3,0},{4,5},{5,6},{6,7},{7,4},{8,9},{9,10},{10,1... | collective-permute-start | bytes 98312 | tf_op jit(solution)/shard_map/ppermute | solution.py:15
  99.5 2.1 %collective-permute-start.11 = (f32[2,2,2,16,128]{4,1,0,3,2:T(2,128)S(1)}, f32[2,2,2,16,128]{4,1,0,3,2:T(2,128)S(1)}, u32[]{:S(2)}, u32[]{:S(2)}) collective-permute-start(f32[2,2,2,16,128]{4,1,0,3,2:T(2,128)S(1)} %bitcast.366), channel_id=1, source_target_pairs={{0,4},{4,8},{8,12},{12,16},{16,20},{20,24},{24,28},{28,32},{32,36}... | collective-permute-start | bytes 196616 | tf_op jit(solution)/shard_map/ppermute | solution.py:15
  103.4 3.6 %collective-permute-done.11 = f32[2,2,2,16,128]{4,1,0,3,2:T(2,128)S(1)} collective-permute-done((f32[2,2,2,16,128]{4,1,0,3,2:T(2,128)S(1)}, f32[2,2,2,16,128]{4,1,0,3,2:T(2,128)S(1)}, u32[]{:S(2)}, u32[]{:S(2)}) %collective-permute-start.11) | collective-permute-done | bytes 65568 | tf_op jit(solution)/shard_map/ppermute | solution.py:15
  108.3 1.3 fusion.5
  110.7 2.4 %fusion.3 = f32[2,2,3,8,16,128]{5,1,0,4,2,3:T(2,128)S(1)} fusion(f32[2,1,3,8,16,128]{5,1,0,4,2,3:T(1,128)S(1)} %get-tuple-element.40, f32[2,1,3,8,16,128]{5,1,0,4,2,3:T(1,128)S(1)} %get-tuple-element.39, f32[2,1,3,8,16,128]{5,1,0,4,2,3:T(1,128)S(1)} %get-tuple-element.25, f32[2,1,3,8,16,128]{5,1,0,4,2,3:T(1,128)S(1)} %get-tuple-element.24, ...), kind=kLoop, calls=%fused_computation.7 | loop fusion | flops 1179648 | bytes 3932160 | tf_op jit(solution)/shard_map/add | solution.py:116
  116.2 21.1 %all-gather = f32[64,16,128]{2,1,0:T(8,128)S(1)} all-gather(f32[8,16,128]{2,1,0:T(8,128)S(1)} %broadcast_select_fusion), channel_id=2, replica_groups=mesh['angle'=8,'gx'=16,'gy'=4] {'angle'}, dimensions={0}, use_global_device_ids=true | all-gather | bytes 589824 | tf_op jit(solution)/shard_map/all_gather | solution.py:124
  (167 shorter events, 38.5 us)
Async XLA Ops:
  0.6 1.4 copy-start.9
  2.9 19.6 %copy-start.10 = (f32[8,2]{0,1:T(2,128)S(1)}, f32[8,2]{0,1:T(2,128)}, u32[]{:S(2)}) copy-start(f32[8,2]{0,1:T(2,128)} %param.14) | copy-start | bytes 196
  2.9 36.1 %collective-permute-start = (f32[2,2,2,8,128]{4,1,0,3,2:T(2,128)}, f32[2,2,2,8,128]{4,1,0,3,2:T(2,128)}, u32[]{:S(2)}, u32[]{:S(2)}) collective-permute-start(f32[2,2,2,8,128]{4,1,0,3,2:T(2,128)} %pad_maximum_fusion.1), channel_id=1, source_target_pairs={{0,3},{1,0},{2,1},{3,2},{4,7},{5,4},{6,5},{7,6},{8,11},{9,8},{10,9... | collective-permute-start | bytes 98312 | tf_op jit(solution)/shard_map/ppermute | solution.py:15
  15.7 25.0 %collective-permute-start.1 = (f32[2,2,2,16,128]{4,1,0,3,2:T(2,128)}, f32[2,2,2,16,128]{4,1,0,3,2:T(2,128)S(1)}, u32[]{:S(2)}, u32[]{:S(2)}) collective-permute-start(f32[2,2,2,16,128]{4,1,0,3,2:T(2,128)} %slice_bitcast_fusion.25), channel_id=1, source_target_pairs={{0,60},{4,0},{8,4},{12,8},{16,12},{20,16},{24,20},{28,24},{32,28},... | collective-permute-start | bytes 196616 | tf_op jit(solution)/shard_map/ppermute | solution.py:15
  21.8 5.4 %copy-start = (f32[2,2,1,8,16,128]{5,4,3,2,1,0:T(8,128)}, f32[2,2,1,8,16,128]{5,4,3,2,1,0:T(8,128)S(1)}, u32[]{:S(2)}) copy-start(f32[2,2,1,8,16,128]{5,4,3,2,1,0:T(8,128)S(1)} %get-tuple-element.49) | copy-start | bytes 786436
  21.8 5.3 %copy-start.2 = (f32[2,2,8,16,128]{4,1,0,3,2:T(2,128)}, f32[2,2,8,16,128]{4,1,0,3,2:T(2,128)S(1)}, u32[]{:S(2)}) copy-start(f32[2,2,8,16,128]{4,1,0,3,2:T(2,128)S(1)} %slice_bitcast_fusion.21) | copy-start | bytes 786436
  25.7 1.5 %copy-start.4 = (f32[2,2,8,16,128]{4,1,0,3,2:T(2,128)}, f32[2,2,8,16,128]{4,1,0,3,2:T(2,128)S(1)}, u32[]{:S(2)}) copy-start(f32[2,2,8,16,128]{4,1,0,3,2:T(2,128)S(1)} %get-tuple-element.112) | copy-start | bytes 786436
  32.5 5.4 %copy-start.3 = (f32[2,2,8,16,128]{4,1,0,3,2:T(2,128)S(1)}, f32[2,2,8,16,128]{4,1,0,3,2:T(2,128)}, u32[]{:S(2)}) copy-start(f32[2,2,8,16,128]{4,1,0,3,2:T(2,128)} %copy-done.2) | copy-start | bytes 786436
  38.9 3.5 %copy-start.1 = (f32[2,2,1,8,16,128]{5,4,3,2,1,0:T(8,128)S(1)}, f32[2,2,1,8,16,128]{5,4,3,2,1,0:T(8,128)}, u32[]{:S(2)}) copy-start(f32[2,2,1,8,16,128]{5,4,3,2,1,0:T(8,128)} %copy-done) | copy-start | bytes 786436
  38.9 3.5 %copy-start.5 = (f32[2,2,8,16,127]{4,1,0,3,2:T(2,128)S(1)}, f32[2,2,8,16,127]{4,1,0,3,2:T(2,128)}, u32[]{:S(2)}) copy-start(f32[2,2,8,16,127]{4,1,0,3,2:T(2,128)} %slice.554) | copy-start | bytes 780292
  38.9 3.5 %copy-start.6 = (f32[2,2,8,16,127]{4,1,0,3,2:T(2,128)S(1)}, f32[2,2,8,16,127]{4,1,0,3,2:T(2,128)}, u32[]{:S(2)}) copy-start(f32[2,2,8,16,127]{4,1,0,3,2:T(2,128)} %slice.556) | copy-start | bytes 780292
  38.9 3.5 %copy-start.7 = (f32[2,2,8,15,128]{4,1,0,3,2:T(2,128)S(1)}, f32[2,2,8,15,128]{4,1,0,3,2:T(2,128)}, u32[]{:S(2)}) copy-start(f32[2,2,8,15,128]{4,1,0,3,2:T(2,128)} %slice.547) | copy-start | bytes 737284
  38.9 3.5 %copy-start.8 = (f32[2,2,7,16,128]{4,1,0,3,2:T(2,128)S(1)}, f32[2,2,7,16,128]{4,1,0,3,2:T(2,128)}, u32[]{:S(2)}) copy-start(f32[2,2,7,16,128]{4,1,0,3,2:T(2,128)} %slice.557) | copy-start | bytes 688132
  44.3 9.2 %collective-permute-start.3 = (f32[2,2,2,16,128]{4,1,0,3,2:T(2,128)S(1)}, f32[2,2,2,16,128]{4,1,0,3,2:T(2,128)S(1)}, u32[]{:S(2)}, u32[]{:S(2)}) collective-permute-start(f32[2,2,2,16,128]{4,1,0,3,2:T(2,128)S(1)} %slice_bitcast_fusion.24), channel_id=1, source_target_pairs={{0,4},{4,8},{8,12},{12,16},{16,20},{20,24},{24,28},{28,32},{32,36}... | collective-permute-start | bytes 196616 | tf_op jit(solution)/shard_map/ppermute | solution.py:15
  46.3 7.1 %collective-permute-start.2 = (f32[2,2,2,8,128]{4,1,0,3,2:T(2,128)S(1)}, f32[2,2,2,8,128]{4,1,0,3,2:T(2,128)S(1)}, u32[]{:S(2)}, u32[]{:S(2)}) collective-permute-start(f32[2,2,2,8,128]{4,1,0,3,2:T(2,128)S(1)} %pad_maximum_fusion.2), channel_id=1, source_target_pairs={{0,1},{1,2},{2,3},{3,0},{4,5},{5,6},{6,7},{7,4},{8,9},{9,10},{10,1... | collective-permute-start | bytes 98312 | tf_op jit(solution)/shard_map/ppermute | solution.py:15
  57.2 8.1 %collective-permute-start.4 = (f32[2,2,2,8,128]{4,1,0,3,2:T(2,128)S(1)}, f32[2,2,2,8,128]{4,1,0,3,2:T(2,128)S(1)}, u32[]{:S(2)}, u32[]{:S(2)}) collective-permute-start(f32[2,2,2,8,128]{4,1,0,3,2:T(2,128)S(1)} %pad_maximum_fusion.3), channel_id=1, source_target_pairs={{0,3},{1,0},{2,1},{3,2},{4,7},{5,4},{6,5},{7,6},{8,11},{9,8},{10,9... | collective-permute-start | bytes 98312 | tf_op jit(solution)/shard_map/ppermute | solution.py:15
  59.9 6.5 %collective-permute-start.5 = (f32[2,2,2,16,128]{4,1,0,3,2:T(2,128)S(1)}, f32[2,2,2,16,128]{4,1,0,3,2:T(2,128)S(1)}, u32[]{:S(2)}, u32[]{:S(2)}) collective-permute-start(f32[2,2,2,16,128]{4,1,0,3,2:T(2,128)S(1)} %slice_bitcast_fusion.23), channel_id=1, source_target_pairs={{0,60},{4,0},{8,4},{12,8},{16,12},{20,16},{24,20},{28,24},{32,28},... | collective-permute-start | bytes 196616 | tf_op jit(solution)/shard_map/ppermute | solution.py:15
  69.5 6.8 %collective-permute-start.6 = (f32[2,2,2,8,128]{4,3,2,1,0:T(8,128)S(1)}, f32[2,2,2,8,128]{4,3,2,1,0:T(8,128)S(1)}, u32[]{:S(2)}, u32[]{:S(2)}) collective-permute-start(f32[2,2,2,8,128]{4,3,2,1,0:T(8,128)S(1)} %pad_maximum_fusion.4), channel_id=1, source_target_pairs={{0,1},{1,2},{2,3},{3,0},{4,5},{5,6},{6,7},{7,4},{8,9},{9,10},{10,1... | collective-permute-start | bytes 98312 | tf_op jit(solution)/shard_map/ppermute | solution.py:15
  73.7 7.5 %collective-permute-start.7 = (f32[2,2,2,16,128]{4,1,0,3,2:T(2,128)S(1)}, f32[2,2,2,16,128]{4,1,0,3,2:T(2,128)S(1)}, u32[]{:S(2)}, u32[]{:S(2)}) collective-permute-start(f32[2,2,2,16,128]{4,1,0,3,2:T(2,128)S(1)} %bitcast.367), channel_id=1, source_target_pairs={{0,4},{4,8},{8,12},{12,16},{16,20},{20,24},{24,28},{28,32},{32,36}... | collective-permute-start | bytes 196616 | tf_op jit(solution)/shard_map/ppermute | solution.py:15
  85.0 7.5 %collective-permute-start.8 = (f32[2,2,2,8,128]{4,1,0,3,2:T(2,128)S(1)}, f32[2,2,2,8,128]{4,1,0,3,2:T(2,128)S(1)}, u32[]{:S(2)}, u32[]{:S(2)}) collective-permute-start(f32[2,2,2,8,128]{4,1,0,3,2:T(2,128)S(1)} %pad_maximum_fusion.5), channel_id=1, source_target_pairs={{0,3},{1,0},{2,1},{3,2},{4,7},{5,4},{6,5},{7,6},{8,11},{9,8},{10,9... | collective-permute-start | bytes 98312 | tf_op jit(solution)/shard_map/ppermute | solution.py:15
  88.9 5.0 %collective-permute-start.9 = (f32[2,2,2,16,128]{4,1,0,3,2:T(2,128)S(1)}, f32[2,2,2,16,128]{4,1,0,3,2:T(2,128)S(1)}, u32[]{:S(2)}, u32[]{:S(2)}) collective-permute-start(f32[2,2,2,16,128]{4,1,0,3,2:T(2,128)S(1)} %slice_bitcast_fusion.22), channel_id=1, source_target_pairs={{0,60},{4,0},{8,4},{12,8},{16,12},{20,16},{24,20},{28,24},{32,28},... | collective-permute-start | bytes 196616 | tf_op jit(solution)/shard_map/ppermute | solution.py:15
  96.5 6.8 %collective-permute-start.10 = (f32[2,2,2,8,128]{4,3,2,1,0:T(8,128)S(1)}, f32[2,2,2,8,128]{4,3,2,1,0:T(8,128)S(1)}, u32[]{:S(2)}, u32[]{:S(2)}) collective-permute-start(f32[2,2,2,8,128]{4,3,2,1,0:T(8,128)S(1)} %copy.293), channel_id=1, source_target_pairs={{0,1},{1,2},{2,3},{3,0},{4,5},{5,6},{6,7},{7,4},{8,9},{9,10},{10,1... | collective-permute-start | bytes 98312 | tf_op jit(solution)/shard_map/ppermute | solution.py:15
  99.5 7.4 %collective-permute-start.11 = (f32[2,2,2,16,128]{4,1,0,3,2:T(2,128)S(1)}, f32[2,2,2,16,128]{4,1,0,3,2:T(2,128)S(1)}, u32[]{:S(2)}, u32[]{:S(2)}) collective-permute-start(f32[2,2,2,16,128]{4,1,0,3,2:T(2,128)S(1)} %bitcast.366), channel_id=1, source_target_pairs={{0,4},{4,8},{8,12},{12,16},{16,20},{20,24},{24,28},{28,32},{32,36}... | collective-permute-start | bytes 196616 | tf_op jit(solution)/shard_map/ppermute | solution.py:15
